TPU v7x, 32 devices: a whole 2x2x4 slice. The times are simulated.
32 devices in a mesh: seq: 8 (over z, x), head: 4 (over y, core).
Axes of the slice: x: 2, y: 2, z: 4, core: 2. Of those that a mesh axis runs over, the one named last changes fastest.
Arguments:
- video_query: bfloat16 [4096, 3072], P(('seq', 'head')), may hold values from -16 to 16
- audio_key: bfloat16 [4096, 3072], P(('seq', 'head')), may hold values from -16 to 16
- audio_value: bfloat16 [4096, 3072], P(('seq', 'head')), may hold values from -6 to 6
- grad_out: bfloat16 [4096, 3072], P(('seq', 'head')), may hold values from -6 to 6
- audio_time: int32 [4096], P(('seq', 'head')), may hold values from -1 to 4999, as said below
Outputs:
- attended: bfloat16 [4096, 3072], P(('seq', 'head'))
- grad_query: bfloat16 [4096, 3072], P(('seq', 'head'))
- grad_key: bfloat16 [4096, 3072], P(('seq', 'head'))
- grad_value: bfloat16 [4096, 3072], P(('seq', 'head'))
Inputs may be any that keep to these rules, and one draw needn't show every extreme that they name: `audio_time`: slots r * 512 to (r+1) * 512 - 1 belong to time range r: their live slots come first, with stamps from r * 625 to (r+1) * 625 - 1 in rising order, and the rest hold -1. Every range has at least 170 live slots, and in every draw some range has all 512 live.
All inputs are finite; a program needn't handle non-finite values.
Results may differ from a plain program's by a relative error of at most 0.0061.
Values may be sent and summed in bfloat16 or wider, within the bound.
A program may use at most 192 MiB of HBM per device.

v0:
```python
import functools

import jax
import jax.numpy as jnp
from jax import lax
from jax.experimental import pallas as pl
from jax.experimental.pallas import tpu as pltpu
from jax.sharding import PartitionSpec as P

DH = 128
SHARD_MS = 625
RADIUS_MS = 1000
NEG_FILL = -1e30
FAR = 1 << 30
LOG2E = 1.4426950408889634
F32 = jnp.float32
BF16 = jnp.bfloat16
NT = (((1,), (1,)), ((), ()))
NN = (((1,), (0,)), ((), ()))
TN = (((0,), (0,)), ((), ()))


def mm(a, b, dims):
    return lax.dot_general(a, b, dims, preferred_element_type=F32)


def attend_half(half, size, block, q_ref, g_ref, k_ref, v_ref, qt_ref, lo_ref, hi_ref, o_ref,
                dq_ref, dk_acc, dv_acc, s_scr):
    scaling = DH ** (-0.5)

    def q_block(step, carry):
        rows = pl.ds(pl.multiple_of(half * size + step * block, block), block)
        q = q_ref[rows, :]
        g = g_ref[rows, :]
        stamp = qt_ref[rows, :]
        top = jnp.full((block, 1), -jnp.inf, F32)
        for j in range(5):
            cols = slice((half + j) * size, (half + j + 1) * size)
            s = mm(q, k_ref[cols, :], NT)
            if j <= 2:
                allowed = lo_ref[:, cols] >= stamp - RADIUS_MS
            else:
                allowed = hi_ref[:, cols] <= stamp + RADIUS_MS
            s = jnp.where(allowed, s, NEG_FILL)
            s_scr[:, j * size:(j + 1) * size] = s
            top = jnp.maximum(top, jnp.max(s, axis=1, keepdims=True))
        total = jnp.zeros((block, 1), F32)
        for j in range(5):
            here = slice(j * size, (j + 1) * size)
            p = jnp.exp2((s_scr[:, here] - top) * (scaling * LOG2E))
            s_scr[:, here] = p
            total = total + jnp.sum(p, axis=1, keepdims=True)
        inverse = 1.0 / total
        out = jnp.zeros((block, DH), F32)
        for j in range(5):
            here = slice(j * size, (j + 1) * size)
            cols = slice((half + j) * size, (half + j + 1) * size)
            weight = s_scr[:, here] * inverse
            s_scr[:, here] = weight
            low = weight.astype(BF16)
            out = out + mm(low, v_ref[cols, :], NN)
            dv_acc[cols, :] += mm(low, g, TN)
        o_ref[rows, :] = out.astype(BF16)
        row_dot = jnp.sum(g.astype(F32) * out, axis=1, keepdims=True)
        dq = jnp.zeros((block, DH), F32)
        for j in range(5):
            here = slice(j * size, (j + 1) * size)
            cols = slice((half + j) * size, (half + j + 1) * size)
            dp = mm(g, v_ref[cols, :], NT)
            ds = (s_scr[:, here] * (dp - row_dot)).astype(BF16)
            dq = dq + mm(ds, k_ref[cols, :], NN)
            dk_acc[cols, :] += mm(ds, q, TN)
        dq_ref[rows, :] = (dq * scaling).astype(BF16)
        return carry

    lax.fori_loop(0, size // block, q_block, 0)


def whole_kernel(blocks, width, heads, size, block,
                 k_in, v_in, q_in, g_in, t_in,
                 o_out, dq_out, dk_out, dv_out,
                 qt_ref, kwin, vwin, qs, gs, tw, lo, hi, o_st, dq_st, psend, prec, fin, center,
                 dk_acc, dv_acc, s_scr,
                 in_send, in_recv, in_local, t_send, t_recv, t_local,
                 halo_send, halo_recv, th_send, th_recv, part_send, part_recv,
                 out_send, out_recv, out_local):
    scaling = DH ** (-0.5)
    group = 2 * width
    seq = lax.axis_index("seq")
    head = lax.axis_index("head")
    blk = seq // 2
    me = (seq % 2) * width + head
    rows = k_in.shape[0]
    span = 2 * size
    has_low = blk > 0
    has_up = blk < blocks - 1
    mid = pl.ds(span, span)

    def peer(p):
        return (blk * 2 + p // width, p % width)

    low_dev = (seq - 2, head)
    up_dev = (seq + 2, head)

    def remote(src, dst, send, recv, dev):
        return pltpu.make_async_remote_copy(
            src_ref=src, dst_ref=dst, send_sem=send, recv_sem=recv, device_id=dev,
            device_id_type=pl.DeviceIdType.MESH)

    def each_peer(action):
        def step(d, carry):
            action((me + d) % group)
            return carry
        lax.fori_loop(1, group, step, 0)

    def wait_bytes(ref, sem):
        pltpu.make_async_copy(ref, ref, sem).wait()

    barrier = pltpu.get_barrier_semaphore()

    def greet(dev):
        pl.semaphore_signal(barrier, inc=1, device_id=dev, device_id_type=pl.DeviceIdType.MESH)

    each_peer(lambda p: greet(peer(p)))

    @pl.when(has_low)
    def _():
        greet(low_dev)

    @pl.when(has_up)
    def _():
        greet(up_dev)

    pl.semaphore_wait(barrier, group - 1 + has_low.astype(jnp.int32) + has_up.astype(jnp.int32))

    ins = (k_in, v_in, q_in, g_in)

    def landing(a, h, p):
        base = span if a < 2 else 0
        where = pl.ds(pl.multiple_of(base + p * rows, rows), rows)
        return (kwin, vwin, qs, gs)[a].at[h, where]

    def columns(p, h):
        return pl.ds(pl.multiple_of((p * heads + h) * DH, DH), DH)

    def spread(arrays, h):
        for a in arrays:
            pltpu.make_async_copy(ins[a].at[:, columns(me, h)], landing(a, h, me),
                                  in_local.at[a, h]).start()

        def send(p):
            for a in arrays:
                remote(ins[a].at[:, columns(p, h)], landing(a, h, me), in_send.at[a],
                       in_recv.at[a, h], peer(p)).start()
        each_peer(send)

    def arrived(a, h):
        ref = (kwin, vwin, qs, gs)[a]
        wait_bytes(ref.at[h, pl.ds(0, (group - 1) * rows)], in_recv.at[a, h])
        wait_bytes(ref.at[h, pl.ds(0, rows)], in_local.at[a, h])

    pltpu.make_async_copy(t_in, tw.at[group + me], t_local).start()
    each_peer(lambda p: remote(t_in, tw.at[group + me], t_send, t_recv, peer(p)).start())
    def halo_up(a, h):
        ref = (kwin, vwin)[a]
        return remote(ref.at[h, mid], ref.at[h, pl.ds(0, span)], halo_send.at[0, a, h],
                      halo_recv.at[0, a, h], up_dev)

    def halo_down(a, h):
        ref = (kwin, vwin)[a]
        return remote(ref.at[h, mid], ref.at[h, pl.ds(2 * span, span)], halo_send.at[1, a, h],
                      halo_recv.at[1, a, h], low_dev)

    def chunk(part, p):
        return pl.ds(pl.multiple_of(part * span + p * rows, rows), rows)

    def chunk_up(a, h, p, src):
        ref = (kwin, vwin)[a]

        @pl.when(has_up)
        def _():
            remote(src, ref.at[h, chunk(0, p)], halo_send.at[0, a, h], halo_recv.at[0, a, h],
                   up_dev).start()

    def chunk_down(a, h, p, src):
        ref = (kwin, vwin)[a]

        @pl.when(has_low)
        def _():
            remote(src, ref.at[h, chunk(2, p)], halo_send.at[1, a, h], halo_recv.at[1, a, h],
                   low_dev).start()

    def own_halo(h):
        for a in range(2):
            src = ins[a].at[:, columns(me, h)]
            chunk_up(a, h, me, src)
            chunk_down(a, h, me, src)

    spread((0, 1), 0)
    for h in range(heads):
        own_halo(h)
    spread((2, 3), 0)
    for h in range(1, heads):
        spread((0, 1), h)
    for h in range(1, heads):
        spread((2, 3), h)

    def t_up():
        return remote(tw.at[pl.ds(group, group)], tw.at[pl.ds(0, group)], th_send.at[0],
                      th_recv.at[0], up_dev)

    def t_down():
        return remote(tw.at[pl.ds(group, group)], tw.at[pl.ds(2 * group, group)], th_send.at[1],
                      th_recv.at[1], low_dev)

    def forward(h):
        for a in range(2):
            arrived(a, h)
            ref = (kwin, vwin)[a]

            def pass_on(p, a=a, ref=ref):
                chunk_up(a, h, p, ref.at[h, chunk(1, p)])
                chunk_down(a, h, p, ref.at[h, chunk(1, p)])
            each_peer(pass_on)

    @pl.when(jnp.logical_not(has_low))
    def _():
        kwin[:, 0:span, :] = jnp.zeros((heads, span, DH), BF16)
        vwin[:, 0:span, :] = jnp.zeros((heads, span, DH), BF16)
        tw[0:group] = jnp.full((group, 1, rows), -1, jnp.int32)

    @pl.when(jnp.logical_not(has_up))
    def _():
        kwin[:, 2 * span:3 * span, :] = jnp.zeros((heads, span, DH), BF16)
        vwin[:, 2 * span:3 * span, :] = jnp.zeros((heads, span, DH), BF16)
        tw[2 * group:3 * group] = jnp.full((group, 1, rows), -1, jnp.int32)

    place = lax.broadcasted_iota(jnp.int32, (size, 1), 0)
    offset = lax.div(place * SHARD_MS, jnp.full((size, 1), size, jnp.int32))
    qt_ref[0:size, :] = offset
    qt_ref[size:span, :] = offset + SHARD_MS

    wait_bytes(tw.at[pl.ds(0, group - 1)], t_recv)
    wait_bytes(tw.at[0], t_local)

    @pl.when(has_up)
    def _():
        t_up().start()

    @pl.when(has_low)
    def _():
        t_down().start()

    forward(0)
    if heads > 1:
        forward(1)

    @pl.when(has_low)
    def _():
        t_up().wait_recv()

    @pl.when(has_up)
    def _():
        t_down().wait_recv()

    first = blk * 2 * SHARD_MS
    for i in range(3 * group):
        t = tw[i]
        here = slice(i * rows, (i + 1) * rows)
        lo[:, here] = jnp.where(t >= 0, t - first, -FAR)
        hi[:, here] = jnp.where(t >= 0, t - first, FAR)

    outs = (o_out, dq_out, dk_out, dv_out)

    def collect(i, src, h):
        pltpu.make_async_copy(src.at[pl.ds(pl.multiple_of(me * rows, rows), rows)],
                              outs[i].at[:, columns(me, h)], out_local.at[i, h]).start()
        each_peer(lambda p: remote(
            src.at[pl.ds(pl.multiple_of(p * rows, rows), rows)],
            outs[i].at[:, columns(me, h)], out_send.at[i], out_recv.at[i], peer(p)).start())

    def part_down(a, h):
        return remote(psend.at[0, a, h], prec.at[0, a, h], part_send.at[0, a, h],
                      part_recv.at[0, a, h], low_dev)

    def part_up(a, h):
        return remote(psend.at[1, a, h], prec.at[1, a, h], part_send.at[1, a, h],
                      part_recv.at[1, a, h], up_dev)

    def finish(h):
        for a in range(2):
            @pl.when(has_up)
            def _(a=a):
                part_down(a, h).wait_recv()
                center[a, h] = center[a, h] + prec[0, a, h].astype(F32)

            @pl.when(has_low)
            def _(a=a):
                part_up(a, h).wait_recv()
                center[a, h] = center[a, h] + prec[1, a, h].astype(F32)

            fin[a, h] = center[a, h].astype(BF16)
            collect(2 + a, fin.at[a, h], h)

    def one_head(h, carry):
        for a in range(2):
            @pl.when(has_low)
            def _(a=a):
                halo_up(a, h).wait_recv()

            @pl.when(has_up)
            def _(a=a):
                halo_down(a, h).wait_recv()
        arrived(2, h)
        arrived(3, h)
        dk_acc[...] = jnp.zeros_like(dk_acc)
        dv_acc[...] = jnp.zeros_like(dv_acc)
        refs = (size, block, qs.at[h], gs.at[h], kwin.at[h], vwin.at[h], qt_ref, lo, hi,
                o_st.at[h], dq_st.at[h], dk_acc, dv_acc, s_scr)
        attend_half(0, *refs)

        @pl.when(h + 2 < heads)
        def _():
            forward(h + 2)

        attend_half(1, *refs)
        for a, (acc, factor) in enumerate(((dk_acc, scaling), (dv_acc, None))):
            def part(i, acc=acc, factor=factor):
                x = acc[i * span:(i + 1) * span, :]
                return x if factor is None else x * factor

            @pl.when(has_low)
            def _(a=a, part=part):
                psend[0, a, h] = part(0).astype(BF16)
                part_down(a, h).start()

            @pl.when(has_up)
            def _(a=a, part=part):
                psend[1, a, h] = part(2).astype(BF16)
                part_up(a, h).start()

            center[a, h] = part(1)
        collect(0, o_st.at[h], h)
        collect(1, dq_st.at[h], h)

        @pl.when(h > 0)
        def _():
            finish(h - 1)
        return carry

    lax.fori_loop(0, heads, one_head, 0)
    finish(heads - 1)

    sent = (group - 1) * heads * DH
    wait_bytes(tw.at[pl.ds(0, group - 1)], t_send)
    for a in range(4):
        wait_bytes(ins[a].at[:, pl.ds(0, sent)], in_send.at[a])
        wait_bytes(outs[a].at[:, pl.ds(0, sent)], out_send.at[a])
        wait_bytes(outs[a].at[:, pl.ds(0, sent)], out_recv.at[a])
        for h in range(heads):
            wait_bytes(outs[a].at[:, pl.ds(0, DH)], out_local.at[a, h])

    @pl.when(has_up)
    def _():
        t_up().wait_send()
        for a in range(2):
            for h in range(heads):
                halo_up(a, h).wait_send()
                part_up(a, h).wait_send()

    @pl.when(has_low)
    def _():
        t_down().wait_send()
        for a in range(2):
            for h in range(heads):
                halo_down(a, h).wait_send()
                part_down(a, h).wait_send()


def hand_over(*refs):
    srcs, dsts, (bufs, in_sem, out_sem) = refs[:4], refs[4:8], refs[8:]
    loads = [pltpu.make_async_copy(srcs[i], bufs.at[i], in_sem.at[i]) for i in range(4)]
    stores = [pltpu.make_async_copy(bufs.at[i], dsts[i], out_sem.at[i]) for i in range(4)]
    for load in loads:
        load.start()
    for load, store in zip(loads, stores):
        load.wait()
        store.start()
    for store in stores:
        store.wait()


def on_device(seq_count, head_count, video_query, audio_key, audio_value, grad_out, audio_time):
    group = 2 * head_count
    rows, features = video_query.shape
    size = rows * head_count
    span = 2 * size
    heads = features // DH // group
    block = min(512, size)
    hbm = pl.BlockSpec(memory_space=pl.ANY)
    dma = pltpu.SemaphoreType.DMA
    pairs = heads * span * 5 * size
    o, dq, dk, dv = pl.pallas_call(
        functools.partial(whole_kernel, seq_count // 2, head_count, heads, size, block),
        in_specs=[hbm] * 5,
        out_specs=[hbm] * 4,
        out_shape=[jax.ShapeDtypeStruct((rows, features), BF16)] * 4,
        scratch_shapes=[
            pltpu.VMEM((span, 1), jnp.int32),
            pltpu.VMEM((heads, 3 * span, DH), BF16),
            pltpu.VMEM((heads, 3 * span, DH), BF16),
            pltpu.VMEM((heads, span, DH), BF16),
            pltpu.VMEM((heads, span, DH), BF16),
            pltpu.VMEM((3 * group, 1, rows), jnp.int32),
            pltpu.VMEM((1, 3 * span), jnp.int32),
            pltpu.VMEM((1, 3 * span), jnp.int32),
            pltpu.VMEM((heads, span, DH), BF16),
            pltpu.VMEM((heads, span, DH), BF16),
            pltpu.VMEM((2, 2, heads, span, DH), BF16),
            pltpu.VMEM((2, 2, heads, span, DH), BF16),
            pltpu.VMEM((2, heads, span, DH), BF16),
            pltpu.VMEM((2, heads, span, DH), F32),
            pltpu.VMEM((3 * span, DH), F32),
            pltpu.VMEM((3 * span, DH), F32),
            pltpu.VMEM((block, 5 * size), F32),
            dma((4,)), dma((4, heads)), dma((4, heads)), dma, dma, dma,
            dma((2, 2, heads)), dma((2, 2, heads)), dma((2,)), dma((2,)),
            dma((2, 2, heads)), dma((2, 2, heads)),
            dma((4,)), dma((4,)), dma((4, heads)),
        ],
        compiler_params=pltpu.CompilerParams(
            collective_id=0, has_side_effects=True, vmem_limit_bytes=56 * 1024 * 1024),
        cost_estimate=pl.CostEstimate(flops=12 * pairs * DH, bytes_accessed=16 * rows * features,
                                      transcendentals=pairs),
    )(audio_key, audio_value, video_query, grad_out, audio_time[None, :])
    return pl.pallas_call(
        hand_over, in_specs=[hbm] * 4, out_specs=[hbm] * 4,
        out_shape=[jax.ShapeDtypeStruct((rows, features), BF16)] * 4,
        scratch_shapes=[pltpu.VMEM((4, rows, features), BF16), dma((4,)), dma((4,))],
    )(o, dq, dk, dv)


def solution(mesh):
    rows = P(("seq", "head"), None)
    return jax.shard_map(
        functools.partial(on_device, mesh.shape["seq"], mesh.shape["head"]),
        mesh=mesh,
        in_specs=(rows, rows, rows, rows, P(("seq", "head"))),
        out_specs=(rows, rows, rows, rows),
        check_vma=False,
    )
```

profile of v0, /device:TPU:0, one launch (start us, length us, event | category | flops | bytes accessed | tf_op | source)
XLA Modules:
  0.0 91.1 jit_solution(11198288867832295257)
XLA Ops:
  0.6 87.6 %shard_map.84 = (bf16[128,3072]{1,0:T(8,128)(2,1)}, bf16[128,3072]{1,0:T(8,128)(2,1)}, bf16[128,3072]{1,0:T(8,128)(2,1)}, bf16[128,3072]{1,0:T(8,128)(2,1)}) custom-call(bf16[128,3072]{1,0:T(8,128)(2,1)} %k_in.1, bf16[128,3072]{1,0:T(8,128)(2,1)} %v_in.1, bf16[128,3072]{1,0:T(8,128)(2,1)} %q_in.1, bf16[128,3072]{1,0:T(8,128)(2,1)} %g_in.1, s32[1,128]{1,0:T(1,128)} %bitcast.1), custom_call_target="tpu_custom_call" | custom-call | flops 12079595520 | bytes 6291456 | tf_op jit(solution)/shard_map/pallas_call | solution.py:403
  88.2 2.9 %shard_map.85 = (bf16[128,3072]{1,0:T(8,128)(2,1)}, bf16[128,3072]{1,0:T(8,128)(2,1)}, bf16[128,3072]{1,0:T(8,128)(2,1)}, bf16[128,3072]{1,0:T(8,128)(2,1)}) custom-call(bf16[128,3072]{1,0:T(8,128)(2,1)} %get-tuple-element.8.refs_0_, bf16[128,3072]{1,0:T(8,128)(2,1)} %get-tuple-element.9.refs_1_, bf16[128,3072]{1,0:T(8,128)(2,1)} %get-tuple-element.10.refs_2_, ...), custom_call_target="tpu_custom_call" | custom-call | tf_op jit(solution)/shard_map/pallas_call | solution.py:436
where the time goes:
time: 91.2 us; the launch traced here: 91.1 us
  Pallas kernels  90.4 us (99%)
    pallas_call x1, Pallas kernels, on_device(): pl.pallas_call(functools.partial(whole_kernel, seq_count // 2, head_count...  87.6 us
    pallas_call x1, Pallas kernels, on_device(): pl.pallas_call(hand_over, in_specs=[hbm] * 4, out_specs=[hbm] * 4, out_sh...  2.86 us

commit v1 on v0

--- a/solution.py
+++ b/solution.py
@@ -199,11 +199,12 @@
     spread((0, 1), 0)
     for h in range(heads):
         own_halo(h)
-    spread((2, 3), 0)
-    for h in range(1, heads):
-        spread((0, 1), h)
-    for h in range(1, heads):
+    if heads > 1:
+        spread((0, 1), 1)
+    for h in range(heads):
         spread((2, 3), h)
+        if h + 2 < heads:
+            spread((0, 1), h + 2)
 
     def t_up():
         return remote(tw.at[pl.ds(group, group)], tw.at[pl.ds(0, group)], th_send.at[0],
@@ -272,35 +273,59 @@
 
     outs = (o_out, dq_out, dk_out, dv_out)
 
-    def collect(i, src, h):
-        pltpu.make_async_copy(src.at[pl.ds(pl.multiple_of(me * rows, rows), rows)],
-                              outs[i].at[:, columns(me, h)], out_local.at[i, h]).start()
-        each_peer(lambda p: remote(
-            src.at[pl.ds(pl.multiple_of(p * rows, rows), rows)],
-            outs[i].at[:, columns(me, h)], out_send.at[i], out_recv.at[i], peer(p)).start())
-
-    def part_down(a, h):
-        return remote(psend.at[0, a, h], prec.at[0, a, h], part_send.at[0, a, h],
-                      part_recv.at[0, a, h], low_dev)
-
-    def part_up(a, h):
-        return remote(psend.at[1, a, h], prec.at[1, a, h], part_send.at[1, a, h],
-                      part_recv.at[1, a, h], up_dev)
+    def piece(p):
+        return pl.ds(pl.multiple_of(p * rows, rows), rows)
+
+    def hand_back(i, src, h, p):
+        @pl.when(p == me)
+        def _():
+            pltpu.make_async_copy(src.at[piece(me)], outs[i].at[:, columns(me, h)],
+                                  out_local.at[i, h]).start()
+
+        @pl.when(p != me)
+        def _():
+            remote(src.at[piece(p)], outs[i].at[:, columns(me, h)], out_send.at[i],
+                   out_recv.at[i], peer(p)).start()
+
+    def collect(half, h):
+        for i, src in enumerate((o_st, dq_st)):
+            def step(d, carry, i=i, src=src):
+                hand_back(i, src.at[h], h, half * width + (head + d) % width)
+                return carry
+            lax.fori_loop(0, width, step, 0)
+
+    def part_down(a, h, p):
+        return remote(psend.at[0, a, h, piece(p)], prec.at[0, a, h, piece(p)],
+                      part_send.at[0, a, h], part_recv.at[0, a, h, p], low_dev)
+
+    def part_up(a, h, p):
+        return remote(psend.at[1, a, h, piece(p)], prec.at[1, a, h, piece(p)],
+                      part_send.at[1, a, h], part_recv.at[1, a, h, p], up_dev)
+
+    def every_piece(action):
+        def step(d, carry):
+            action((me + d) % group)
+            return carry
+        lax.fori_loop(0, group, step, 0)
 
     def finish(h):
         for a in range(2):
-            @pl.when(has_up)
-            def _(a=a):
-                part_down(a, h).wait_recv()
-                center[a, h] = center[a, h] + prec[0, a, h].astype(F32)
-
-            @pl.when(has_low)
-            def _(a=a):
-                part_up(a, h).wait_recv()
-                center[a, h] = center[a, h] + prec[1, a, h].astype(F32)
-
-            fin[a, h] = center[a, h].astype(BF16)
-            collect(2 + a, fin.at[a, h], h)
+            def one(p, a=a):
+                here = piece(p)
+
+                @pl.when(has_up)
+                def _():
+                    part_down(a, h, p).wait_recv()
+                    center[a, h, here] = center[a, h, here] + prec[0, a, h, here].astype(F32)
+
+                @pl.when(has_low)
+                def _():
+                    part_up(a, h, p).wait_recv()
+                    center[a, h, here] = center[a, h, here] + prec[1, a, h, here].astype(F32)
+
+                fin[a, h, here] = center[a, h, here].astype(BF16)
+                hand_back(2 + a, fin.at[a, h], h, p)
+            every_piece(one)
 
     def one_head(h, carry):
         for a in range(2):
@@ -318,10 +343,15 @@
         refs = (size, block, qs.at[h], gs.at[h], kwin.at[h], vwin.at[h], qt_ref, lo, hi,
                 o_st.at[h], dq_st.at[h], dk_acc, dv_acc, s_scr)
         attend_half(0, *refs)
+        collect(0, h)
 
         @pl.when(h + 2 < heads)
         def _():
             forward(h + 2)
+
+        @pl.when(h >= 2)
+        def _():
+            finish(h - 2)
 
         attend_half(1, *refs)
         for a, (acc, factor) in enumerate(((dk_acc, scaling), (dv_acc, None))):
@@ -332,24 +362,24 @@
             @pl.when(has_low)
             def _(a=a, part=part):
                 psend[0, a, h] = part(0).astype(BF16)
-                part_down(a, h).start()
+                every_piece(lambda p: part_down(a, h, p).start())
 
             @pl.when(has_up)
             def _(a=a, part=part):
                 psend[1, a, h] = part(2).astype(BF16)
-                part_up(a, h).start()
+                every_piece(lambda p: part_up(a, h, p).start())
 
             center[a, h] = part(1)
-        collect(0, o_st.at[h], h)
-        collect(1, dq_st.at[h], h)
-
-        @pl.when(h > 0)
-        def _():
-            finish(h - 1)
+        collect(1, h)
         return carry
 
     lax.fori_loop(0, heads, one_head, 0)
-    finish(heads - 1)
+
+    def settle(h, carry):
+        finish(h)
+        return carry
+
+    lax.fori_loop(max(heads - 2, 0), heads, settle, 0)
 
     sent = (group - 1) * heads * DH
     wait_bytes(tw.at[pl.ds(0, group - 1)], t_send)
@@ -366,7 +396,7 @@
         for a in range(2):
             for h in range(heads):
                 halo_up(a, h).wait_send()
-                part_up(a, h).wait_send()
+                wait_bytes(psend.at[1, a, h], part_send.at[1, a, h])
 
     @pl.when(has_low)
     def _():
@@ -374,7 +404,7 @@
         for a in range(2):
             for h in range(heads):
                 halo_down(a, h).wait_send()
-                part_down(a, h).wait_send()
+                wait_bytes(psend.at[0, a, h], part_send.at[0, a, h])
 
 
 def hand_over(*refs):
@@ -425,7 +455,7 @@
             pltpu.VMEM((block, 5 * size), F32),
             dma((4,)), dma((4, heads)), dma((4, heads)), dma, dma, dma,
             dma((2, 2, heads)), dma((2, 2, heads)), dma((2,)), dma((2,)),
-            dma((2, 2, heads)), dma((2, 2, heads)),
+            dma((2, 2, heads)), dma((2, 2, heads, group)),
             dma((4,)), dma((4,)), dma((4, heads)),
         ],
         compiler_params=pltpu.CompilerParams(

time: 91.2 us -> 85.5 us (0.938)
  Pallas kernels: 90.4 us -> 84 us
    pallas_call x1, Pallas kernels: 87.6 us -> 81.1 us  [on_device(): pl.pallas_call(functools.partial(whole_kernel, seq_count // 2, head_count...]
where the time goes in v1:
time: 85.5 us; the launch traced here: 84.6 us
  Pallas kernels  84 us (98%)
    pallas_call x1, Pallas kernels, on_device(): pl.pallas_call(functools.partial(whole_kernel, seq_count // 2, head_count...  81.1 us
    pallas_call x1, Pallas kernels, on_device(): pl.pallas_call(hand_over, in_specs=[hbm] * 4, out_specs=[hbm] * 4, out_sh...  2.86 us

profile of v1, /device:TPU:0, one launch (start us, length us, event | category | flops | bytes accessed | tf_op | source)
XLA Modules:
  0.0 84.6 jit_solution(17934162732591654897)
XLA Ops:
  0.6 81.1 %shard_map.84 = (bf16[128,3072]{1,0:T(8,128)(2,1)}, bf16[128,3072]{1,0:T(8,128)(2,1)}, bf16[128,3072]{1,0:T(8,128)(2,1)}, bf16[128,3072]{1,0:T(8,128)(2,1)}) custom-call(bf16[128,3072]{1,0:T(8,128)(2,1)} %k_in.1, bf16[128,3072]{1,0:T(8,128)(2,1)} %v_in.1, bf16[128,3072]{1,0:T(8,128)(2,1)} %q_in.1, bf16[128,3072]{1,0:T(8,128)(2,1)} %g_in.1, s32[1,128]{1,0:T(1,128)} %bitcast.1), custom_call_target="tpu_custom_call" | custom-call | flops 12079595520 | bytes 6291456 | tf_op jit(solution)/shard_map/pallas_call | solution.py:433
  81.7 2.9 %shard_map.85 = (bf16[128,3072]{1,0:T(8,128)(2,1)}, bf16[128,3072]{1,0:T(8,128)(2,1)}, bf16[128,3072]{1,0:T(8,128)(2,1)}, bf16[128,3072]{1,0:T(8,128)(2,1)}) custom-call(bf16[128,3072]{1,0:T(8,128)(2,1)} %get-tuple-element.8.refs_0_, bf16[128,3072]{1,0:T(8,128)(2,1)} %get-tuple-element.9.refs_1_, bf16[128,3072]{1,0:T(8,128)(2,1)} %get-tuple-element.10.refs_2_, ...), custom_call_target="tpu_custom_call" | custom-call | tf_op jit(solution)/shard_map/pallas_call | solution.py:466

commit v2 on v1

--- a/solution.py
+++ b/solution.py
@@ -24,64 +24,59 @@
     return lax.dot_general(a, b, dims, preferred_element_type=F32)
 
 
-def attend_half(half, size, block, q_ref, g_ref, k_ref, v_ref, qt_ref, lo_ref, hi_ref, o_ref,
-                dq_ref, dk_acc, dv_acc, s_scr):
+def attend_half(half, size, q_ref, g_ref, k_ref, v_ref, qt_ref, lo_ref, hi_ref, o_ref,
+                dq_ref, emit, s_scr):
     scaling = DH ** (-0.5)
-
-    def q_block(step, carry):
-        rows = pl.ds(pl.multiple_of(half * size + step * block, block), block)
-        q = q_ref[rows, :]
-        g = g_ref[rows, :]
-        stamp = qt_ref[rows, :]
-        top = jnp.full((block, 1), -jnp.inf, F32)
-        for j in range(5):
-            cols = slice((half + j) * size, (half + j + 1) * size)
-            s = mm(q, k_ref[cols, :], NT)
-            if j <= 2:
-                allowed = lo_ref[:, cols] >= stamp - RADIUS_MS
-            else:
-                allowed = hi_ref[:, cols] <= stamp + RADIUS_MS
-            s = jnp.where(allowed, s, NEG_FILL)
-            s_scr[:, j * size:(j + 1) * size] = s
-            top = jnp.maximum(top, jnp.max(s, axis=1, keepdims=True))
-        total = jnp.zeros((block, 1), F32)
-        for j in range(5):
-            here = slice(j * size, (j + 1) * size)
-            p = jnp.exp2((s_scr[:, here] - top) * (scaling * LOG2E))
-            s_scr[:, here] = p
-            total = total + jnp.sum(p, axis=1, keepdims=True)
-        inverse = 1.0 / total
-        out = jnp.zeros((block, DH), F32)
-        for j in range(5):
-            here = slice(j * size, (j + 1) * size)
-            cols = slice((half + j) * size, (half + j + 1) * size)
-            weight = s_scr[:, here] * inverse
-            s_scr[:, here] = weight
-            low = weight.astype(BF16)
-            out = out + mm(low, v_ref[cols, :], NN)
-            dv_acc[cols, :] += mm(low, g, TN)
-        o_ref[rows, :] = out.astype(BF16)
-        row_dot = jnp.sum(g.astype(F32) * out, axis=1, keepdims=True)
-        dq = jnp.zeros((block, DH), F32)
-        for j in range(5):
-            here = slice(j * size, (j + 1) * size)
-            cols = slice((half + j) * size, (half + j + 1) * size)
-            dp = mm(g, v_ref[cols, :], NT)
-            ds = (s_scr[:, here] * (dp - row_dot)).astype(BF16)
-            dq = dq + mm(ds, k_ref[cols, :], NN)
-            dk_acc[cols, :] += mm(ds, q, TN)
-        dq_ref[rows, :] = (dq * scaling).astype(BF16)
-        return carry
-
-    lax.fori_loop(0, size // block, q_block, 0)
-
-
-def whole_kernel(blocks, width, heads, size, block,
+    rows = slice(half * size, (half + 1) * size)
+    q = q_ref[rows, :]
+    g = g_ref[rows, :]
+    stamp = qt_ref[rows, :]
+    top = jnp.full((size, 1), -jnp.inf, F32)
+    for j in range(5):
+        cols = slice((half + j) * size, (half + j + 1) * size)
+        s = mm(q, k_ref[cols, :], NT)
+        if j <= 2:
+            allowed = lo_ref[:, cols] >= stamp - RADIUS_MS
+        else:
+            allowed = hi_ref[:, cols] <= stamp + RADIUS_MS
+        s = jnp.where(allowed, s, NEG_FILL)
+        s_scr[:, j * size:(j + 1) * size] = s
+        top = jnp.maximum(top, jnp.max(s, axis=1, keepdims=True))
+    total = jnp.zeros((size, 1), F32)
+    for j in range(5):
+        here = slice(j * size, (j + 1) * size)
+        p = jnp.exp2((s_scr[:, here] - top) * (scaling * LOG2E))
+        s_scr[:, here] = p
+        total = total + jnp.sum(p, axis=1, keepdims=True)
+    inverse = 1.0 / total
+    out = jnp.zeros((size, DH), F32)
+    for j in range(5):
+        here = slice(j * size, (j + 1) * size)
+        cols = slice((half + j) * size, (half + j + 1) * size)
+        weight = s_scr[:, here] * inverse
+        s_scr[:, here] = weight
+        low = weight.astype(BF16)
+        out = out + mm(low, v_ref[cols, :], NN)
+        emit(1, half, j, mm(low, g, TN))
+    o_ref[rows, :] = out.astype(BF16)
+    row_dot = jnp.sum(g.astype(F32) * out, axis=1, keepdims=True)
+    dq = jnp.zeros((size, DH), F32)
+    for j in range(5):
+        here = slice(j * size, (j + 1) * size)
+        cols = slice((half + j) * size, (half + j + 1) * size)
+        dp = mm(g, v_ref[cols, :], NT)
+        ds = (s_scr[:, here] * (dp - row_dot)).astype(BF16)
+        dq = dq + mm(ds, k_ref[cols, :], NN)
+        emit(0, half, j, mm(ds, q, TN))
+    dq_ref[rows, :] = (dq * scaling).astype(BF16)
+
+
+def whole_kernel(blocks, width, heads, size,
                  k_in, v_in, q_in, g_in, t_in,
                  o_out, dq_out, dk_out, dv_out,
                  qt_ref, kwin, vwin, qs, gs, tw, lo, hi, o_st, dq_st, psend, prec, fin, center,
-                 dk_acc, dv_acc, s_scr,
-                 in_send, in_recv, in_local, t_send, t_recv, t_local,
+                 acc, s_scr,
+                 in_send, in_recv, near_recv, in_local, t_send, t_recv, t_local,
                  halo_send, halo_recv, th_send, th_recv, part_send, part_recv,
                  out_send, out_recv, out_local):
     scaling = DH ** (-0.5)
@@ -113,6 +108,23 @@
             return carry
         lax.fori_loop(1, group, step, 0)
 
+    partner = me // 2 * 2 + (me + 1) % 2
+
+    chips = group // 2
+    chip = me // 2
+
+    def each_far_chip(action):
+        def step(d, carry):
+            action((chip + d) % chips)
+            return carry
+        lax.fori_loop(1, chips, step, 0)
+
+    def each_far(action):
+        def both(c):
+            action(c * 2)
+            action(c * 2 + 1)
+        each_far_chip(both)
+
     def wait_bytes(ref, sem):
         pltpu.make_async_copy(ref, ref, sem).wait()
 
@@ -152,11 +164,18 @@
             for a in arrays:
                 remote(ins[a].at[:, columns(p, h)], landing(a, h, me), in_send.at[a],
                        in_recv.at[a, h], peer(p)).start()
-        each_peer(send)
+        if arrays[0] == 0:
+            each_far(send)
+        else:
+            each_peer(send)
+
+    def near(a, h):
+        return remote(ins[a].at[:, columns(partner, h)], landing(a, h, me), in_send.at[a],
+                      near_recv.at[a, h], peer(partner))
 
     def arrived(a, h):
         ref = (kwin, vwin, qs, gs)[a]
-        wait_bytes(ref.at[h, pl.ds(0, (group - 1) * rows)], in_recv.at[a, h])
+        wait_bytes(ref.at[h, pl.ds(0, (group - (2 if a < 2 else 1)) * rows)], in_recv.at[a, h])
         wait_bytes(ref.at[h, pl.ds(0, rows)], in_local.at[a, h])
 
     pltpu.make_async_copy(t_in, tw.at[group + me], t_local).start()
@@ -196,6 +215,9 @@
             chunk_up(a, h, me, src)
             chunk_down(a, h, me, src)
 
+    for h in range(heads):
+        for a in range(2):
+            near(a, h).start()
     spread((0, 1), 0)
     for h in range(heads):
         own_halo(h)
@@ -214,15 +236,34 @@
         return remote(tw.at[pl.ds(group, group)], tw.at[pl.ds(2 * group, group)], th_send.at[1],
                       th_recv.at[1], low_dev)
 
+    def pair(part, c):
+        return pl.ds(pl.multiple_of(part * span + c * 2 * rows, 2 * rows), 2 * rows)
+
     def forward(h):
         for a in range(2):
             arrived(a, h)
             ref = (kwin, vwin)[a]
 
-            def pass_on(p, a=a, ref=ref):
-                chunk_up(a, h, p, ref.at[h, chunk(1, p)])
-                chunk_down(a, h, p, ref.at[h, chunk(1, p)])
-            each_peer(pass_on)
+            def pass_on(c, a=a, ref=ref):
+                src = ref.at[h, pair(1, c)]
+
+                @pl.when(has_up)
+                def _():
+                    remote(src, ref.at[h, pair(0, c)], halo_send.at[0, a, h],
+                           halo_recv.at[0, a, h], up_dev).start()
+
+                @pl.when(has_low)
+                def _():
+                    remote(src, ref.at[h, pair(2, c)], halo_send.at[1, a, h],
+                           halo_recv.at[1, a, h], low_dev).start()
+            each_far_chip(pass_on)
+
+    for h in range(heads):
+        for a in range(2):
+            near(a, h).wait_recv()
+            src = (kwin, vwin)[a].at[h, chunk(1, partner)]
+            chunk_up(a, h, partner, src)
+            chunk_down(a, h, partner, src)
 
     @pl.when(jnp.logical_not(has_low))
     def _():
@@ -294,38 +335,66 @@
                 return carry
             lax.fori_loop(0, width, step, 0)
 
-    def part_down(a, h, p):
-        return remote(psend.at[0, a, h, piece(p)], prec.at[0, a, h, piece(p)],
-                      part_send.at[0, a, h], part_recv.at[0, a, h, p], low_dev)
-
-    def part_up(a, h, p):
-        return remote(psend.at[1, a, h, piece(p)], prec.at[1, a, h, piece(p)],
-                      part_send.at[1, a, h], part_recv.at[1, a, h, p], up_dev)
-
-    def every_piece(action):
-        def step(d, carry):
-            action((me + d) % group)
-            return carry
-        lax.fori_loop(0, group, step, 0)
+    def both_pieces(c):
+        return pl.ds(pl.multiple_of(c * 2 * rows, 2 * rows), 2 * rows)
+
+    def part_down(a, h, c):
+        return remote(psend.at[0, a, h, both_pieces(c)], prec.at[0, a, h, both_pieces(c)],
+                      part_send.at[0, a, h], part_recv.at[0, a, h, c], low_dev)
+
+    def part_up(a, h, c):
+        return remote(psend.at[1, a, h, both_pieces(c)], prec.at[1, a, h, both_pieces(c)],
+                      part_send.at[1, a, h], part_recv.at[1, a, h, c], up_dev)
+
+    def early_parts(h):
+        @pl.when(has_low)
+        def _():
+            for a in (1, 0):
+                for c in range(chips // 2):
+                    part_down(a, h, c).start()
+
+    def late_parts(h):
+        for a in (1, 0):
+            @pl.when(has_low)
+            def _(a=a):
+                for c in range(chips // 2, chips):
+                    part_down(a, h, c).start()
+
+            @pl.when(has_up)
+            def _(a=a):
+                each_far_chip(lambda c: part_up(a, h, c).start())
+                part_up(a, h, chip).start()
 
     def finish(h):
-        for a in range(2):
-            def one(p, a=a):
-                here = piece(p)
+        for a in (1, 0):
+            def add(c, a=a):
+                here = both_pieces(c)
 
                 @pl.when(has_up)
                 def _():
-                    part_down(a, h, p).wait_recv()
+                    part_down(a, h, c).wait_recv()
                     center[a, h, here] = center[a, h, here] + prec[0, a, h, here].astype(F32)
 
                 @pl.when(has_low)
                 def _():
-                    part_up(a, h, p).wait_recv()
+                    part_up(a, h, c).wait_recv()
                     center[a, h, here] = center[a, h, here] + prec[1, a, h, here].astype(F32)
 
                 fin[a, h, here] = center[a, h, here].astype(BF16)
-                hand_back(2 + a, fin.at[a, h], h, p)
-            every_piece(one)
+
+            def send(p, a=a):
+                remote(fin.at[a, h, piece(p)], outs[2 + a].at[:, columns(me, h)],
+                       out_send.at[2 + a], out_recv.at[2 + a], peer(p)).start()
+
+            def one(c, a=a):
+                add(c)
+                send(c * 2)
+                send(c * 2 + 1)
+            each_far_chip(one)
+            add(chip)
+            send(partner)
+            pltpu.make_async_copy(fin.at[a, h, piece(me)], outs[2 + a].at[:, columns(me, h)],
+                                  out_local.at[2 + a, h]).start()
 
     def one_head(h, carry):
         for a in range(2):
@@ -338,10 +407,24 @@
                 halo_down(a, h).wait_recv()
         arrived(2, h)
         arrived(3, h)
-        dk_acc[...] = jnp.zeros_like(dk_acc)
-        dv_acc[...] = jnp.zeros_like(dv_acc)
-        refs = (size, block, qs.at[h], gs.at[h], kwin.at[h], vwin.at[h], qt_ref, lo, hi,
-                o_st.at[h], dq_st.at[h], dk_acc, dv_acc, s_scr)
+
+        def emit(a, half, j, x):
+            spot = half + j
+            if half == 0 and j > 0:
+                acc[a, (j - 1) * size:j * size, :] = x
+                return
+            if half == 1 and j < 4:
+                x = acc[a, j * size:(j + 1) * size, :] + x
+            if a == 0:
+                x = x * scaling
+            there = slice(spot % 2 * size, (spot % 2 + 1) * size)
+            if spot // 2 == 1:
+                center[a, h, there] = x
+            else:
+                psend[spot // 4, a, h, there] = x.astype(BF16)
+
+        refs = (size, qs.at[h], gs.at[h], kwin.at[h], vwin.at[h], qt_ref, lo, hi,
+                o_st.at[h], dq_st.at[h], emit, s_scr)
         attend_half(0, *refs)
         collect(0, h)
 
@@ -349,27 +432,14 @@
         def _():
             forward(h + 2)
 
+        early_parts(h)
+
         @pl.when(h >= 2)
         def _():
             finish(h - 2)
 
         attend_half(1, *refs)
-        for a, (acc, factor) in enumerate(((dk_acc, scaling), (dv_acc, None))):
-            def part(i, acc=acc, factor=factor):
-                x = acc[i * span:(i + 1) * span, :]
-                return x if factor is None else x * factor
-
-            @pl.when(has_low)
-            def _(a=a, part=part):
-                psend[0, a, h] = part(0).astype(BF16)
-                every_piece(lambda p: part_down(a, h, p).start())
-
-            @pl.when(has_up)
-            def _(a=a, part=part):
-                psend[1, a, h] = part(2).astype(BF16)
-                every_piece(lambda p: part_up(a, h, p).start())
-
-            center[a, h] = part(1)
+        late_parts(h)
         collect(1, h)
         return carry
 
@@ -408,13 +478,9 @@
 
 
 def hand_over(*refs):
-    srcs, dsts, (bufs, in_sem, out_sem) = refs[:4], refs[4:8], refs[8:]
-    loads = [pltpu.make_async_copy(srcs[i], bufs.at[i], in_sem.at[i]) for i in range(4)]
-    stores = [pltpu.make_async_copy(bufs.at[i], dsts[i], out_sem.at[i]) for i in range(4)]
-    for load in loads:
-        load.start()
-    for load, store in zip(loads, stores):
-        load.wait()
+    srcs, dsts, sem = refs[:4], refs[4:8], refs[8]
+    stores = [pltpu.make_async_copy(srcs[i], dsts[i], sem.at[i]) for i in range(4)]
+    for store in stores:
         store.start()
     for store in stores:
         store.wait()
@@ -426,15 +492,15 @@
     size = rows * head_count
     span = 2 * size
     heads = features // DH // group
-    block = min(512, size)
     hbm = pl.BlockSpec(memory_space=pl.ANY)
+    vmem = pl.BlockSpec(memory_space=pltpu.VMEM)
     dma = pltpu.SemaphoreType.DMA
     pairs = heads * span * 5 * size
     o, dq, dk, dv = pl.pallas_call(
-        functools.partial(whole_kernel, seq_count // 2, head_count, heads, size, block),
-        in_specs=[hbm] * 5,
-        out_specs=[hbm] * 4,
-        out_shape=[jax.ShapeDtypeStruct((rows, features), BF16)] * 4,
+        functools.partial(whole_kernel, seq_count // 2, head_count, heads, size),
+        in_specs=[pl.BlockSpec(memory_space=pltpu.HBM)] * 5,
+        out_specs=[vmem] * 4,
+        out_shape=[pltpu.VMEM((rows, features), BF16)] * 4,
         scratch_shapes=[
             pltpu.VMEM((span, 1), jnp.int32),
             pltpu.VMEM((heads, 3 * span, DH), BF16),
@@ -450,23 +516,23 @@
             pltpu.VMEM((2, 2, heads, span, DH), BF16),
             pltpu.VMEM((2, heads, span, DH), BF16),
             pltpu.VMEM((2, heads, span, DH), F32),
-            pltpu.VMEM((3 * span, DH), F32),
-            pltpu.VMEM((3 * span, DH), F32),
-            pltpu.VMEM((block, 5 * size), F32),
-            dma((4,)), dma((4, heads)), dma((4, heads)), dma, dma, dma,
+            pltpu.VMEM((2, 4 * size, DH), F32),
+            pltpu.VMEM((size, 5 * size), F32),
+            dma((4,)), dma((4, heads)), dma((2, heads)), dma((4, heads)), dma, dma, dma,
             dma((2, 2, heads)), dma((2, 2, heads)), dma((2,)), dma((2,)),
-            dma((2, 2, heads)), dma((2, 2, heads, group)),
+            dma((2, 2, heads)), dma((2, 2, heads, head_count)),
             dma((4,)), dma((4,)), dma((4, heads)),
         ],
         compiler_params=pltpu.CompilerParams(
-            collective_id=0, has_side_effects=True, vmem_limit_bytes=56 * 1024 * 1024),
+            collective_id=0, has_side_effects=True, vmem_limit_bytes=52 * 1024 * 1024),
         cost_estimate=pl.CostEstimate(flops=12 * pairs * DH, bytes_accessed=16 * rows * features,
                                       transcendentals=pairs),
     )(audio_key, audio_value, video_query, grad_out, audio_time[None, :])
     return pl.pallas_call(
         hand_over, in_specs=[hbm] * 4, out_specs=[hbm] * 4,
         out_shape=[jax.ShapeDtypeStruct((rows, features), BF16)] * 4,
-        scratch_shapes=[pltpu.VMEM((4, rows, features), BF16), dma((4,)), dma((4,))],
+        scratch_shapes=[dma((4,))],
+        compiler_params=pltpu.CompilerParams(vmem_limit_bytes=4 * 1024 * 1024),
     )(o, dq, dk, dv)
 
 

time: 85.5 us -> 81.8 us (0.957)
  Pallas kernels: 84 us -> 81 us
    pallas_call x1, Pallas kernels: 81.1 us -> 79.3 us  [on_device(): pl.pallas_call(functools.partial(whole_kernel, seq_count // 2, head_count...]
    pallas_call x1, Pallas kernels: 2.86 us -> 1.69 us  [on_device(): pl.pallas_call(hand_over, in_specs=[hbm] * 4, out_specs=[hbm] * 4, out_sh...]
where the time goes in v2:
time: 81.8 us; the launch traced here: 81.7 us
  Pallas kernels  81 us (99%)
    pallas_call x1, Pallas kernels, on_device(): pl.pallas_call(functools.partial(whole_kernel, seq_count // 2, head_count...  79.3 us
    pallas_call x1, Pallas kernels, on_device(): pl.pallas_call(hand_over, in_specs=[hbm] * 4, out_specs=[hbm] * 4, out_sh...  1.69 us

profile of v2, /device:TPU:0, one launch (start us, length us, event | category | flops | bytes accessed | tf_op | source)
XLA Modules:
  0.0 81.7 jit_solution(12287815302748116888)
XLA Ops:
  0.6 79.3 %shard_map.84 = (bf16[128,3072]{1,0:T(8,128)(2,1)S(1)}, bf16[128,3072]{1,0:T(8,128)(2,1)S(1)}, bf16[128,3072]{1,0:T(8,128)(2,1)S(1)}, bf16[128,3072]{1,0:T(8,128)(2,1)S(1)}) custom-call(bf16[128,3072]{1,0:T(8,128)(2,1)} %k_in.1, bf16[128,3072]{1,0:T(8,128)(2,1)} %v_in.1, bf16[128,3072]{1,0:T(8,128)(2,1)} %q_in.1, bf16[128,3072]{1,0:T(8,128)(2,1)} %g_in.1, ...), custom_call_target="tpu_custom_call" | custom-call | flops 12079595520 | bytes 6291456 | tf_op jit(solution)/shard_map/pallas_call | solution.py:499
  80.0 1.7 %shard_map.85 = (bf16[128,3072]{1,0:T(8,128)(2,1)}, bf16[128,3072]{1,0:T(8,128)(2,1)}, bf16[128,3072]{1,0:T(8,128)(2,1)}, bf16[128,3072]{1,0:T(8,128)(2,1)}) custom-call(bf16[128,3072]{1,0:T(8,128)(2,1)S(1)} %get-tuple-element.8.refs_0_, bf16[128,3072]{1,0:T(8,128)(2,1)S(1)} %get-tuple-element.9.refs_1_, bf16[128,3072]{1,0:T(8,128)(2,1)S(1)} %get-tuple-element.10.refs_2_, ...), custom_call_target="tpu_custom_call" | custom-call | tf_op jit(solution)/shard_map/pallas_call | solution.py:531

commit v3 on v2

--- a/solution.py
+++ b/solution.py
@@ -346,19 +346,12 @@
         return remote(psend.at[1, a, h, both_pieces(c)], prec.at[1, a, h, both_pieces(c)],
                       part_send.at[1, a, h], part_recv.at[1, a, h, c], up_dev)
 
-    def early_parts(h):
-        @pl.when(has_low)
-        def _():
-            for a in (1, 0):
-                for c in range(chips // 2):
-                    part_down(a, h, c).start()
-
-    def late_parts(h):
+    def send_parts(h):
         for a in (1, 0):
             @pl.when(has_low)
             def _(a=a):
-                for c in range(chips // 2, chips):
-                    part_down(a, h, c).start()
+                each_far_chip(lambda c: part_down(a, h, c).start())
+                part_down(a, h, chip).start()
 
             @pl.when(has_up)
             def _(a=a):
@@ -432,14 +425,12 @@
         def _():
             forward(h + 2)
 
-        early_parts(h)
-
         @pl.when(h >= 2)
         def _():
             finish(h - 2)
 
         attend_half(1, *refs)
-        late_parts(h)
+        send_parts(h)
         collect(1, h)
         return carry
 

time: 81.8 us -> 81.2 us (level)
  no operation moved by 1% of the time
where the time goes in v3:
time: 81.2 us; the launch traced here: 81 us
  Pallas kernels  80.4 us (99%)
    pallas_call x1, Pallas kernels, on_device(): pl.pallas_call(functools.partial(whole_kernel, seq_count // 2, head_count...  78.7 us
    pallas_call x1, Pallas kernels, on_device(): pl.pallas_call(hand_over, in_specs=[hbm] * 4, out_specs=[hbm] * 4, out_sh...  1.69 us

profile of v3, /device:TPU:0, one launch (start us, length us, event | category | flops | bytes accessed | tf_op | source)
XLA Modules:
  0.0 81.0 jit_solution(6932880174786611439)
XLA Ops:
  0.6 78.7 %shard_map.84 = (bf16[128,3072]{1,0:T(8,128)(2,1)S(1)}, bf16[128,3072]{1,0:T(8,128)(2,1)S(1)}, bf16[128,3072]{1,0:T(8,128)(2,1)S(1)}, bf16[128,3072]{1,0:T(8,128)(2,1)S(1)}) custom-call(bf16[128,3072]{1,0:T(8,128)(2,1)} %k_in.1, bf16[128,3072]{1,0:T(8,128)(2,1)} %v_in.1, bf16[128,3072]{1,0:T(8,128)(2,1)} %q_in.1, bf16[128,3072]{1,0:T(8,128)(2,1)} %g_in.1, ...), custom_call_target="tpu_custom_call" | custom-call | flops 12079595520 | bytes 6291456 | tf_op jit(solution)/shard_map/pallas_call | solution.py:490
  79.3 1.7 %shard_map.85 = (bf16[128,3072]{1,0:T(8,128)(2,1)}, bf16[128,3072]{1,0:T(8,128)(2,1)}, bf16[128,3072]{1,0:T(8,128)(2,1)}, bf16[128,3072]{1,0:T(8,128)(2,1)}) custom-call(bf16[128,3072]{1,0:T(8,128)(2,1)S(1)} %get-tuple-element.8.refs_0_, bf16[128,3072]{1,0:T(8,128)(2,1)S(1)} %get-tuple-element.9.refs_1_, bf16[128,3072]{1,0:T(8,128)(2,1)S(1)} %get-tuple-element.10.refs_2_, ...), custom_call_target="tpu_custom_call" | custom-call | tf_op jit(solution)/shard_map/pallas_call | solution.py:522
